TPU v7x, 128 devices: a whole 4x4x4 slice. The times are simulated.
128 devices in a mesh: row: 16 (over z, y), col: 8 (over x, core).
Axes of the slice: x: 4, y: 4, z: 4, core: 2. Of those that a mesh axis runs over, the one named last changes fastest.
Arguments:
- amplitudes: bfloat16 [16, 4, 1024, 1024], P(None, None, 'row', 'col'), may hold values from -6 to 6
- cycle_integrals: bfloat16 [4, 8, 1024, 1024], P(None, None, 'row', 'col'), may hold values from -0.375 to 0.375
- mask_amp: int32 [16, 16], replicated, may hold values 0 or 1
- mask_int: int32 [16, 16], replicated, may hold values 0 or 1
- occupied_i: float32 [16], P('row'), may hold values from -1 to -0.3
- occupied_j: float32 [8], P('col'), may hold values from -1 to -0.3
- virtual_energy: float32 [1024], replicated, may hold values from 0.2 to 1.5
Outputs:
- update: bfloat16 [16, 8, 1024, 1024], P('row', 'col')
Inputs may be any that keep to these rules, and one draw needn't show every extreme that they name: mask_amp holds 0 or 1: 1 where the amplitude tile survives screening. mask_int holds 0 or 1: 1 where the intermediate tile survives screening.
All inputs are finite; a program needn't handle non-finite values.
Results may differ from a plain program's by a relative error of at most 0.0049.
Values may be sent and summed in bfloat16 or wider, within the bound.
A program may use at most 192 MiB of HBM per device.

v0:
```python
import jax
import jax.numpy as jnp
from jax import lax
from jax.sharding import PartitionSpec as P

TILE = 64


def local_mask(mask, row_first, row_tiles, col_first, col_tiles):
    window = lax.dynamic_slice(mask, (row_first, col_first), (row_tiles, col_tiles))
    return jnp.repeat(jnp.repeat(window, TILE, axis=0), TILE, axis=1).astype(jnp.bfloat16)


def per_device(
    amplitudes, cycle_integrals, mask_amp, mask_int, occupied_i, occupied_j, virtual_energy
):
    row_index = lax.axis_index("row")
    col_index = lax.axis_index("col")
    row_tiles = amplitudes.shape[2] // TILE
    col_tiles = amplitudes.shape[3] // TILE
    amp_masked = (
        amplitudes
        * local_mask(mask_amp, row_index * row_tiles, row_tiles, col_index * col_tiles, col_tiles)[
            None, None
        ]
    )
    int_masked = (
        cycle_integrals
        * local_mask(mask_int, row_index * row_tiles, row_tiles, col_index * col_tiles, col_tiles)[
            None, None
        ]
    )
    whole = virtual_energy.shape[0]
    partial_value = jnp.einsum(
        "ikac,kjbc->ijab",
        amp_masked,
        lax.all_gather(int_masked, "row", axis=2, tiled=True),
        preferred_element_type=jnp.float32,
    )
    exchanged = lax.all_to_all(
        lax.all_to_all(partial_value[None], "row", split_axis=1, concat_axis=3, tiled=True),
        "col",
        split_axis=2,
        concat_axis=0,
        tiled=True,
    )
    cycle = jnp.sum(exchanged, axis=0).astype(jnp.bfloat16)
    denominator = virtual_energy[:, None] + virtual_energy[None, :] - occupied_i[0] - occupied_j[0]
    result = cycle.reshape(whole, whole).astype(jnp.float32) / denominator
    return result.astype(jnp.bfloat16)[None, None]


def solution(mesh):
    in_specs = (
        P(None, None, "row", "col"),
        P(None, None, "row", "col"),
        P(),
        P(),
        P("row"),
        P("col"),
        P(),
    )
    out_specs = P("row", "col", None, None)
    return jax.shard_map(
        per_device, mesh=mesh, in_specs=in_specs, out_specs=out_specs, check_vma=False
    )
```

profile of v0, /device:TPU:1, one launch (start us, length us, event | category | flops | bytes accessed | tf_op | source)
XLA Modules:
  0.0 901.8 jit_solution(1429564766172475192)
XLA Ops:
  6.5 0.0 all-gather.2.cloned.1.call-start
  6.5 0.8 convert_bitcast_fusion
  7.3 0.1 broadcast_in_dim.6
  7.4 0.1 convert_element_type.63
  7.5 1.9 copy_multiply_fusion
  9.4 0.0 all-gather.2.cloned.1.call-update
  9.4 0.1 broadcast_in_dim.7
  9.4 0.1 convert_element_type.66
  9.5 74.1 %all-gather.2.cloned.1.call-done = bf16[4,8,1024,128]{3,2,0,1:T(8,128)(2,1)} async-done(((bf16[4,8,64,128]{3,2,0,1:T(8,128)(2,1)}), bf16[4,8,1024,128]{3,2,0,1:T(8,128)(2,1)}) %all-gather.2.cloned.1.call-update) | async-done | bytes 8388624 | tf_op jit(solution)/shard_map/all_gather | solution.py:37
  83.6 18.9 %convolution_bitcast_fusion = f32[1,16,8,64,1024]{4,3,1,2,0:T(8,128)} fusion(bf16[4,8,1024,128]{3,2,0,1:T(8,128)(2,1)} %all-gather.2.cloned.1.call-done, bf16[16,4,64,128]{3,2,1,0:T(8,128)(2,1)} %param.7, bf16[128]{0:T(256)(128)(2,1)S(1)} %convert_element_type.66), kind=kOutput, calls=%fused_computation | convolution fusion | flops 8592031744 | bytes 42991872 | tf_op jit(solution)/shard_map/ikac,kjbc->ijab/dot_general | solution.py:34
  102.5 12.1 %copy.12 = f32[1,16,8,64,1024]{4,3,2,0,1:T(8,128)S(1)} copy(f32[1,16,8,64,1024]{4,3,1,2,0:T(8,128)} %convolution_bitcast_fusion) | data formatting | bytes 67108864 | tf_op jit(solution)/shard_map/broadcast_in_dim | solution.py:41
  114.6 369.3 %all_to_all.27 = f32[1,16,8,64,1024]{4,3,2,0,1:T(8,128)} all-to-all(f32[1,16,8,64,1024]{4,3,2,0,1:T(8,128)S(1)} %copy.12), channel_id=1, replica_groups=mesh['row'=16,'col'=8] {'row'}, dimensions={1} | all-to-all | bytes 67108864 | tf_op jit(solution)/shard_map/all_to_all | solution.py:41
  483.9 23.3 %copy.13 = f32[1,16,8,64,1024]{4,3,1,2,0:T(8,128)} copy(f32[1,16,8,64,1024]{4,3,2,0,1:T(8,128)} %all_to_all.27) | data formatting | bytes 67108864 | tf_op jit(solution)/shard_map/all_to_all | solution.py:41
  507.3 9.0 %all-to-all-start.1 = ((f32[1,1,8,1024,1024]{4,3,1,0,2:T(8,128)}), f32[1,1,8,1024,1024]{4,3,1,0,2:T(8,128)}, u32[]{:S(2)}, u32[]{:S(2)}) async-start(f32[1,1,8,1024,1024]{4,3,1,0,2:T(8,128)} %bitcast.33), calls=%async_computation.1 | async-start | bytes 67108864 | tf_op jit(solution)/shard_map/all_to_all | solution.py:40
  517.6 0.0 copy-start
  517.6 362.2 %all-to-all-done.1 = f32[1,1,8,1024,1024]{4,3,1,0,2:T(8,128)} async-done(((f32[1,1,8,1024,1024]{4,3,1,0,2:T(8,128)}), f32[1,1,8,1024,1024]{4,3,1,0,2:T(8,128)}, u32[]{:S(2)}, u32[]{:S(2)}) %all-to-all-start.1) | async-done | bytes 33554464 | tf_op jit(solution)/shard_map/all_to_all | solution.py:40
  879.8 12.9 %reduce_sum.9 = bf16[1024,1024]{1,0:T(8,128)(2,1)S(1)} reduce(f32[1,1,8,1024,1024]{4,3,1,0,2:T(8,128)} %all-to-all-done.1, f32[]{:T(128)} %constant.16.clone.1), dimensions={0,1,2}, to_apply=%region_0.0 | reduce | flops 7340032 | bytes 35651588 | tf_op jit(solution)/shard_map/reduce_sum | solution.py:47
  892.7 0.0 copy-done
  892.7 2.3 fusion.1
Async XLA Ops:
  6.5 77.1 %all-gather.2.cloned.1.call-start = ((), (), s32[]{:S(2)}) async-start(), calls=%async_computation.2 | async-start | bytes 8912896 | tf_op jit(solution)/shard_map/all_gather | solution.py:37
  507.3 372.6 %all-to-all-start.1 = ((f32[1,1,8,1024,1024]{4,3,1,0,2:T(8,128)}), f32[1,1,8,1024,1024]{4,3,1,0,2:T(8,128)}, u32[]{:S(2)}, u32[]{:S(2)}) async-start(f32[1,1,8,1024,1024]{4,3,1,0,2:T(8,128)} %bitcast.33), calls=%async_computation.1 | async-start | bytes 67108864 | tf_op jit(solution)/shard_map/all_to_all | solution.py:40
  517.6 375.1 %copy-start = (f32[1024]{0:T(1024)S(1)}, f32[1024]{0:T(1024)}, u32[]{:S(2)}) copy-start(f32[1024]{0:T(1024)} %param.13) | copy-start | bytes 12292
Sparse Core Ops, SparseCore 0:
  9.5 74.0 all-gather.1
where the time goes:
time: 902 us
  waiting for transfers between devices  436 us (48%)
  blocking collectives  369 us (41%)
  local copies, waits for them, and re-layouts  35.8 us (4%)
  matrix products  18.9 us (2%)
  other arithmetic  17.8 us (2%)
  between operations  14.7 us (2%)
  starting transfers between devices  9.05 us (1%)
    all_to_all x1, blocking collectives, per_device(): lax.all_to_all(partial_value[None], 'row', split_axis=1, concat_axis=3, t...  369 us
    all_to_all x1, waiting for transfers between devices, per_device(): lax.all_to_all(lax.all_to_all(partial_value[None], 'row', split_axis=1, c...  362 us
    all_gather x1, waiting for transfers between devices, per_device(): lax.all_gather(int_masked, 'row', axis=2, tiled=True)  74.1 us
    all_to_all x1, local copies, waits for them, and re-layouts, per_device(): lax.all_to_all(partial_value[None], 'row', split_axis=1, concat_axis=3, t...  23.3 us
    dot_general x1, matrix products, per_device(): jnp.einsum('ikac,kjbc->ijab', amp_masked, lax.all_gather(int_masked, 'row...  18.9 us
  transfers between devices with their start and end apart: 2, of which 2 were waited for; matrix products, arithmetic and copies ran while one was open for 0% of the time, Pallas kernels for 0%

commit v1 on v0

v1 whole, which is shorter than its diff:
```python
import functools

import jax
import jax.numpy as jnp
from jax import lax
from jax.experimental import pallas as pl
from jax.experimental.pallas import tpu as pltpu
from jax.sharding import PartitionSpec as P

TILE = 64
MESH = pl.DeviceIdType.MESH

LEVELS = ((9, 24), (10, 28), (12, 36), (16, 64))


def comm_kernel(
    cap1, cap2, tab, amp, integ, out,
    recv_a, recv_b, grp_b1, ga0, ga1, ga2, ga3, gb0, gb1, gb2, gb3, dense_a, dense_b, acc,
    a1_send, a1_recv, b1_send, b1_recv, ring_send, ring_recv, sib_send, sib_recv,
):
    grp_a, grp_b = (ga0, ga1, ga2, ga3), (gb0, gb1, gb2, gb3)
    row = lax.axis_index("row")
    col = lax.axis_index("col")
    x = col // 2
    core = col % 2
    z = row // 4
    y = row % 4
    p = (1 - core) * y + core * z
    q = (1 - core) * z + core * y
    sp = (1 - core) + core * 4
    sq = (1 - core) * 4 + core

    def row_of(pp, qq):
        return pp * sp + qq * sq

    sibling = (row, 2 * x + 1 - core)

    barrier = pltpu.get_barrier_semaphore()

    def signal(target):
        pl.semaphore_signal(barrier, inc=1, device_id=target, device_id_type=MESH)

    for d in range(1, 16):
        for cc in range(2):
            signal(((row + d) % 16, 2 * x + cc))
    signal(sibling)
    for d in range(1, 4):
        for cc in range(2):
            signal((row, 2 * ((x + d) % 4) + cc))
    pl.semaphore_wait(barrier, 37)

    def b1_copy(d):
        target = (col + d) % 8
        return pltpu.make_async_remote_copy(
            src_ref=integ.at[:, target], dst_ref=recv_b.at[col],
            send_sem=b1_send, recv_sem=b1_recv,
            device_id=(row, target), device_id_type=MESH,
        )

    for d in range(1, 8):
        b1_copy(d).start()
    pltpu.make_async_copy(integ.at[:, col], recv_b.at[col], b1_recv).start()

    def a1_copy(d, cc):
        target = (row + d) % 16
        return pltpu.make_async_remote_copy(
            src_ref=amp.at[target, pl.ds(2 * cc, 2)], dst_ref=recv_a.at[core * 16 + row],
            send_sem=a1_send, recv_sem=a1_recv,
            device_id=(target, 2 * x + cc), device_id_type=MESH,
        )

    for d in range(1, 16):
        for cc in range(2):
            a1_copy(d, cc).start()
    a1_copy(0, 1 - core).start()
    pltpu.make_async_copy(amp.at[row, pl.ds(2 * core, 2)], recv_a.at[core * 16 + row], a1_recv).start()

    for g in range(4):
        grp_a[g][:, cap2] = jnp.zeros((2, TILE, 128), jnp.bfloat16)
        grp_b[g][cap2] = jnp.zeros((2, TILE, 128), jnp.bfloat16)
    half = lax.broadcasted_iota(jnp.int32, (TILE, 128), 1) // TILE

    def mixed(first, second, parity):
        turned = pltpu.roll(second.astype(jnp.float32), TILE, 1)
        return jnp.where(half == parity, first.astype(jnp.float32), turned).astype(jnp.bfloat16)

    def ring(which, buf, pos, cap, target_of):
        right, left = (pos + 1) % 4, (pos + 3) % 4
        cut = cap // 2

        def copy(src, dst, to, k, s, e):
            return pltpu.make_async_remote_copy(
                src_ref=buf(src, s, e), dst_ref=buf(dst, s, e), send_sem=ring_send.at[which, k],
                recv_sem=ring_recv.at[which, k], device_id=target_of(to), device_id_type=MESH,
            )

        return (copy(0, 3, right, 0, 0, cap), copy(0, 1, left, 1, 0, cap),
                copy(3, 2, right, 2, 0, cut), copy(1, 2, left, 3, cut, cap))

    def part(ref, s, e):
        return ref.at[pl.ds(s, e - s)]

    def ring_b1_copies():
        right, left, opp = (p + 1) % 4, (p + 3) % 4, (p + 2) % 4
        cut = cap1 // 2

        def copy(block, to, k, s, e):
            ref = grp_b1.at[block, pl.ds(s, e - s)]
            return pltpu.make_async_remote_copy(
                src_ref=ref, dst_ref=ref, send_sem=ring_send.at[0, k], recv_sem=ring_recv.at[0, k],
                device_id=(row_of(to, q), col), device_id_type=MESH,
            )

        return (copy(p, right, 0, 0, cap1), copy(p, left, 1, 0, cap1),
                copy(left, right, 2, 0, cut), copy(right, left, 3, cut, cap1))

    ring_b1 = ring_b1_copies()
    ring_b2 = ring(1, lambda g, s, e: part(grp_b[g], s, e), q, cap2, lambda to: (row_of(p, to), col))
    ring_a = ring(2, lambda g, s, e: grp_a[g].at[core, pl.ds(s, e - s)], x, cap2,
                  lambda to: (row, 2 * to + core))

    def sib_copy(g):
        ref = grp_a[g].at[core, pl.ds(0, cap2)]
        return pltpu.make_async_remote_copy(
            src_ref=ref, dst_ref=ref, send_sem=sib_send.at[g], recv_sem=sib_recv.at[g],
            device_id=sibling, device_id_type=MESH,
        )

    def sib_arrival(g):
        there = grp_a[g].at[1 - core, pl.ds(0, cap2)]
        return pltpu.make_async_copy(there, there, sib_recv.at[g])

    pltpu.make_async_copy(recv_b, recv_b, b1_recv).wait()

    def pack_b(s, _):
        e = tab[64 + s]
        for kp in range(2):
            grp_b1[p, s, kp] = mixed(recv_b[e // 2, 2 * kp], recv_b[e // 2, 2 * kp + 1], e % 2)
        return 0

    lax.fori_loop(0, cap1, pack_b, 0)
    ring_b1[0].start()
    ring_b1[1].start()

    pltpu.make_async_copy(recv_a, recv_a, a1_recv).wait()

    def pack_a(s, _):
        e = tab[s]
        grp_a[0][core, s] = mixed(recv_a[e // 2, 0], recv_a[e // 2, 1], e % 2)
        return 0

    lax.fori_loop(0, cap2, pack_a, 0)
    ring_a[0].start()
    ring_a[1].start()
    sib_copy(0).start()

    ring_b1[0].wait_recv()
    ring_b1[2].start()
    ring_b1[1].wait_recv()
    ring_b1[3].start()
    ring_b1[2].wait_recv()
    ring_b1[3].wait_recv()

    def pack_b2(s, _):
        e = tab[128 + s]
        grp_b[0][s] = grp_b1[e // 16, e % 16]
        return 0

    lax.fori_loop(0, cap2, pack_b2, 0)
    ring_b2[0].start()
    ring_b2[1].start()

    def expand_a(rel):
        g = (x + rel) % 4

        def body(a, _):
            for cc in range(4):
                slot = jnp.minimum(tab[192 + g * 64 + a * 4 + cc], cap2)
                for kp in range(2):
                    dense_a[g, pl.ds(a * TILE, TILE), pl.ds((2 * cc + kp) * 128, 128)] = grp_a[rel][kp, slot]
            return 0

        lax.fori_loop(0, 16, body, 0)

    def expand_b(rel):
        g = (q + rel) % 4

        def body(pp, _):
            for c in range(16):
                slot = jnp.minimum(tab[448 + g * 64 + pp * 16 + c], cap2)
                for kp in range(2):
                    dense_b[g, c // 4, pl.ds(pp * TILE, TILE), pl.ds(((c % 4) * 2 + kp) * 128, 128)] = (
                        grp_b[rel][slot, kp]
                    )
            return 0

        lax.fori_loop(0, 4, body, 0)

    def product(rel_a, rel_b, first):
        ga, gb = (x + rel_a) % 4, (q + rel_b) % 4

        def body(m, _):
            rows = pl.ds(m * 256, 256)
            part_sum = lax.dot_general(
                dense_a[ga, rows], dense_b[gb, ga], (((1,), (1,)), ((), ())),
                preferred_element_type=jnp.float32,
            )
            if first:
                acc[gb, rows] = part_sum
            else:
                acc[gb, rows] += part_sum
            return 0

        lax.fori_loop(0, 4, body, 0)

    ring_a[0].wait_recv()
    ring_a[2].start()
    sib_copy(3).start()
    ring_a[1].wait_recv()
    ring_a[3].start()
    sib_copy(1).start()

    expand_b(0)
    sib_arrival(0).wait()
    expand_a(0)
    product(0, 0, True)

    ring_a[2].wait_recv()
    ring_a[3].wait_recv()
    sib_copy(2).start()

    ring_b2[0].wait_recv()
    ring_b2[2].start()
    ring_b2[1].wait_recv()
    ring_b2[3].start()

    for rel in (3, 1, 2):
        sib_arrival(rel).wait()
        expand_a(rel)
        product(rel, 0, False)

    def finish(rel_b):
        expand_b(rel_b)
        for rel in (0, 3, 1, 2):
            product(rel, rel_b, rel == 0)

    finish(3)
    finish(1)
    ring_b2[2].wait_recv()
    ring_b2[3].wait_recv()
    finish(2)

    def narrow(t, _):
        rows = pl.ds((t % 8) * 128, 128)
        out[t // 8, rows] = acc[t // 8, rows].astype(jnp.bfloat16)
        return 0

    lax.fori_loop(0, 32, narrow, 0)

    for d in range(1, 8):
        b1_copy(d).wait_send()
    for d in range(1, 16):
        for cc in range(2):
            a1_copy(d, cc).wait_send()
    a1_copy(0, 1 - core).wait_send()
    for r in (ring_b1, ring_b2, ring_a):
        for c in r:
            c.wait_send()
    for g in range(4):
        sib_copy(g).wait_send()


def contract(level, tab, amp, integ):
    cap1, cap2 = LEVELS[level]
    bf16 = jnp.bfloat16
    dma = pltpu.SemaphoreType.DMA
    return pl.pallas_call(
        functools.partial(comm_kernel, cap1, cap2),
        out_shape=jax.ShapeDtypeStruct((4, 1024, 256), bf16),
        in_specs=[
            pl.BlockSpec(memory_space=pltpu.SMEM),
            pl.BlockSpec(memory_space=pl.ANY),
            pl.BlockSpec(memory_space=pl.ANY),
        ],
        out_specs=pl.BlockSpec(memory_space=pltpu.VMEM),
        scratch_shapes=[
            pltpu.VMEM((32, 2, TILE, 128), bf16),
            pltpu.VMEM((8, 4, TILE, 128), bf16),
            pltpu.VMEM((4, cap1, 2, TILE, 128), bf16),
            *[pltpu.VMEM((2, cap2 + 1, TILE, 128), bf16)] * 4,
            *[pltpu.VMEM((cap2 + 1, 2, TILE, 128), bf16)] * 4,
            pltpu.VMEM((4, 1024, 1024), bf16),
            pltpu.VMEM((4, 4, 256, 1024), bf16),
            pltpu.VMEM((4, 1024, 256), jnp.float32),
            dma, dma, dma, dma,
            dma((3, 4)), dma((3, 4)), dma((4,)), dma((4,)),
        ],
        compiler_params=pltpu.CompilerParams(
            collective_id=level + 1, has_side_effects=True, vmem_limit_bytes=60 << 20
        ),
    )(tab, amp, integ)


def tables(mask_amp, mask_int):
    row = lax.axis_index("row")
    col = lax.axis_index("col")
    x = col // 2
    core = col % 2

    def rank(m):
        n = m.shape[-1]
        before = jnp.arange(n)[:, None] < jnp.arange(n)[None, :]
        return jnp.sum(m[..., :, None] * before.astype(jnp.int32), axis=-2)

    def listed(m, ranks, code, n):
        hit = (ranks[:, None] == jnp.arange(n)[None, :]) & (m[:, None] > 0)
        return jnp.sum(jnp.where(hit, code[:, None], 0), axis=0)

    m_a = mask_amp.reshape(16, 4, 4).transpose(1, 0, 2).reshape(4, 64)
    rank_a = rank(m_a)
    t = jnp.arange(64)
    a, cc = t // 4, t % 4
    code_a = ((cc // 2) * 16 + a) * 2 + cc % 2
    pick = lambda v, g: lax.dynamic_index_in_dim(v, g, 0, keepdims=False)
    list_a = listed(pick(m_a, x), pick(rank_a, x), code_a, 64)
    slot_a = jnp.where(m_a > 0, rank_a, 64)

    rank_row = rank(mask_int)
    list_b1 = listed(pick(mask_int, row), pick(rank_row, row), jnp.arange(16), 64)

    by_z = mask_int.reshape(4, 4, 16)
    by_y = by_z.transpose(1, 0, 2)
    rk_z = rank_row.reshape(4, 4, 16)
    rk_y = rk_z.transpose(1, 0, 2)
    m_b = jnp.where(core == 0, by_z, by_y).reshape(4, 64)
    rk = jnp.where(core == 0, rk_z, rk_y).reshape(4, 64)
    q = jnp.where(core == 0, row // 4, row % 4)
    rank_b = rank(m_b)
    list_b2 = listed(pick(m_b, q), pick(rank_b, q), (t // 16) * 16 + pick(rk, q), 64)
    slot_b = jnp.where(m_b > 0, rank_b, 64)

    most1 = jnp.max(jnp.sum(mask_int, axis=1))
    most2 = jnp.maximum(
        jnp.max(jnp.sum(m_a, axis=1)),
        jnp.maximum(jnp.max(jnp.sum(by_z, axis=(1, 2))), jnp.max(jnp.sum(by_y, axis=(1, 2)))),
    )
    level = sum(((most1 > c1) | (most2 > c2)).astype(jnp.int32) for c1, c2 in LEVELS[:-1])
    tab = jnp.concatenate([list_a, list_b1, list_b2, slot_a.reshape(-1), slot_b.reshape(-1)])
    return tab, level


def per_device(
    amplitudes, cycle_integrals, mask_amp, mask_int, occupied_i, occupied_j, virtual_energy
):
    tab, level = tables(mask_amp, mask_int)
    branches = [functools.partial(contract, k) for k in range(len(LEVELS))]
    cycle = lax.switch(level, branches, tab, amplitudes, cycle_integrals)
    core = lax.axis_index("col") % 2
    blocks = cycle.reshape(4, 1024, 4, TILE)
    cycle = jnp.where(core == 0, blocks.transpose(1, 0, 2, 3), blocks.transpose(1, 2, 0, 3)).reshape(1024, 1024)
    denominator = virtual_energy[:, None] + virtual_energy[None, :] - occupied_i[0] - occupied_j[0]
    result = cycle.astype(jnp.float32) / denominator
    return result.astype(jnp.bfloat16)[None, None]


def solution(mesh):
    in_specs = (
        P(None, None, "row", "col"),
        P(None, None, "row", "col"),
        P(),
        P(),
        P("row"),
        P("col"),
        P(),
    )
    out_specs = P("row", "col", None, None)
    return jax.shard_map(
        per_device, mesh=mesh, in_specs=in_specs, out_specs=out_specs, check_vma=False
    )
```

time: 902 us -> 92.5 us (0.10)
  waiting for transfers between devices: 436 us -> 0 us
  blocking collectives: 369 us -> 0 us
  Pallas kernels: 0 us -> 69.1 us
  local copies, waits for them, and re-layouts: 35.8 us -> 8.76 us
  matrix products: 18.9 us -> 0 us
  other arithmetic: 17.8 us -> 8.36 us
  between operations: 14.7 us -> 5.44 us
  starting transfers between devices: 9.05 us -> 0 us
    all_to_all x1 -> x0, blocking collectives: 369 us -> none  [per_device(): lax.all_to_all(partial_value[None], 'row', split_axis=1, concat_axis=3, t...]
    all_to_all x1 -> x0, waiting for transfers between devices: 362 us -> none  [per_device(): lax.all_to_all(lax.all_to_all(partial_value[None], 'row', split_axis=1, c...]
    all_gather x1 -> x0, waiting for transfers between devices: 74.1 us -> none  [per_device(): lax.all_gather(int_masked, 'row', axis=2, tiled=True)]
    pallas_call x0 -> x1, Pallas kernels: none -> 69.1 us  [contract(): pl.pallas_call(functools.partial(comm_kernel, cap1, cap2), out_shape=jax....]
    all_to_all x1 -> x0, local copies, waits for them, and re-layouts: 23.3 us -> none  [per_device(): lax.all_to_all(partial_value[None], 'row', split_axis=1, concat_axis=3, t...]
    dot_general x1 -> x0, matrix products: 18.9 us -> none  [per_device(): jnp.einsum('ikac,kjbc->ijab', amp_masked, lax.all_gather(int_masked, 'row...]
    broadcast_in_dim x3 -> x0, local copies, waits for them, and re-layouts: 12.2 us -> none  [the longest x1 12.1 us: per_device(): partial_value[None]]
    reduce_sum x1 -> x9, other arithmetic: 12.9 us -> 3.03 us  [the longest x2 0.96 us: rank(): return jnp.sum(m[..., :, None] * before.astype(jnp.int32), axis=-2)]
  transfers between devices with their start and end apart: 2 -> 0, of which waited for: 2 -> 0; matrix products, arithmetic and copies ran while one was open for 0% -> 0% of each run, Pallas kernels for 0% -> 0%
where the time goes in v1:
time: 92.5 us; the launch traced here: 91.9 us
  Pallas kernels  69.1 us (75%)
  local copies, waits for them, and re-layouts  8.76 us (9%)
  other arithmetic  8.36 us (9%)
  between operations  5.44 us (6%)
    pallas_call x1, Pallas kernels, contract(): pl.pallas_call(functools.partial(comm_kernel, cap1, cap2), out_shape=jax....  69.1 us
    pallas_call x1, local copies, waits for them, and re-layouts, contract(): pl.pallas_call(functools.partial(comm_kernel, cap1, cap2), out_shape=jax....  2.99 us
    convert_element_type x1, local copies, waits for them, and re-layouts, per_device(): return result.astype(jnp.bfloat16)[None, None]  2.56 us
    unnamed x5, local copies, waits for them, and re-layouts  2.09 us

profile of v1, /device:TPU:1, one launch (start us, length us, event | category | flops | bytes accessed | tf_op | source)
XLA Modules:
  0.0 91.9 jit_solution(13004406370458942026)
XLA Ops:
  0.0 0.8 broadcast_compare_fusion
  0.8 0.1 mul.74
  0.9 0.8 copy.36
  1.6 0.1 copy.37
  1.7 0.1 mul.65
  1.8 0.1 multiply_reduce_fusion
  2.0 0.1 reduce_sum.116
  2.1 0.1 reduce_sum.117
  2.2 0.1 gt.80
  2.3 0.1 copy.40
  2.4 0.1 gt.78
  2.6 0.8 multiply_reduce_fusion.1
  3.4 0.1 reshape.243
  3.5 0.1 select_reduce_fusion
  3.6 0.1 select_reduce_fusion.1
  3.8 0.7 compare_bitcast_fusion.1
  4.5 0.1 select_reduce_fusion.2
  4.6 0.1 concatenate.3
  4.7 0.8 reduce_sum.103
  5.5 0.1 reduce_sum.107
  5.6 0.1 fusion.15
  5.7 0.6 reduce_max.38
  6.3 0.7 reduce_max.39
  8.4 0.7 reduce_sum.104
  9.1 0.1 reduce_sum.105
  9.2 0.1 reduce_sum.106
  9.3 0.6 reduce_max.37
  10.6 0.6 reduce_max.36
  13.2 69.4 %conditional.1 = (bf16[4,1024,256]{2,1,0:T(8,128)(2,1)S(1)}) conditional(s32[]{:T(128)} %clamp.3, (s32[704]{0:T(1024)S(1)}, bf16[16,4,64,128]{3,2,1,0:T(8,128)(2,1)}, bf16[4,8,64,128]{3,2,1,0:T(8,128)(2,1)}) %tuple.35, (s32[704]{0:T(1024)S(1)}, bf16[16,4,64,128]{3,2,1,0:T(8,128)(2,1)}, ...), branch_computations={%region_15.16_spmd, %region_16.17_spmd, %region_17.18_spmd, %regio... | conditional | bytes 8 | solution.py:357
  13.2 69.1 %branch_1_fun.1 = bf16[4,1024,256]{2,1,0:T(8,128)(2,1)S(1)} custom-call(s32[704]{0:T(1024)S(1)} %get-tuple-element.41.tab, bf16[16,4,64,128]{3,2,1,0:T(8,128)(2,1)} %get-tuple-element.60.amp, bf16[4,8,64,128]{3,2,1,0:T(8,128)(2,1)} %get-tuple-element.64.integ), custom_call_target="tpu_custom_call" | custom-call | tf_op jit(solution)/shard_map/cond/branch_1_fun/pallas_call | solution.py:277
  82.6 0.0 copy-start
  82.6 1.3 %copy-done = bf16[4,1024,256]{2,1,0:T(8,128)(2,1)} copy-done((bf16[4,1024,256]{2,1,0:T(8,128)(2,1)}, bf16[4,1024,256]{2,1,0:T(8,128)(2,1)S(1)}, u32[]{:S(2)}) %copy-start) | copy-done | bytes 2097176
  83.9 3.0 %copy.43 = bf16[4,1024,256]{1,2,0:T(8,128)(2,1)S(1)} copy(bf16[4,1024,256]{2,1,0:T(8,128)(2,1)} %copy-done) | data formatting | bytes 4194304 | tf_op jit(solution)/shard_map/cond/branch_0_fun/pallas_call | solution.py:277
  86.9 0.0 copy-start.1
  86.9 0.2 bitcast_select_fusion
  88.4 0.0 copy-done.1
  88.4 0.9 %fusion = bf16[1,1,1024,1024]{2,3,1,0:T(8,128)(2,1)S(1)} fusion(bf16[1024,4,4,64]{0,3,2,1:T(8,128)(2,1)S(1)} %bitcast_select_fusion, f32[]{:T(128)} %bitcast.37, f32[]{:T(128)} %bitcast.36, f32[1024]{0:T(1024)S(1)} %copy-done.1), kind=kLoop, calls=%fused_computation.1 | loop fusion | flops 6291456 | bytes 4198408 | tf_op jit(solution)/shard_map/convert_element_type | solution.py:363
  89.4 2.6 %copy.42 = bf16[1,1,1024,1024]{3,2,1,0:T(8,128)(2,1)} copy(bf16[1,1,1024,1024]{2,3,1,0:T(8,128)(2,1)S(1)} %fusion) | data formatting | bytes 4194304 | tf_op jit(solution)/shard_map/convert_element_type | solution.py:363
  (9 shorter events, 0.1 us)
Async XLA Ops:
  82.6 1.3 %copy-start = (bf16[4,1024,256]{2,1,0:T(8,128)(2,1)}, bf16[4,1024,256]{2,1,0:T(8,128)(2,1)S(1)}, u32[]{:S(2)}) copy-start(bf16[4,1024,256]{2,1,0:T(8,128)(2,1)S(1)} %get-tuple-element.67) | copy-start | bytes 6291460
  86.9 1.5 %copy-start.1 = (f32[1024]{0:T(1024)S(1)}, f32[1024]{0:T(1024)}, u32[]{:S(2)}) copy-start(f32[1024]{0:T(1024)} %param.17) | copy-start | bytes 12292

commit v2 on v0

v2 whole, which is shorter than its diff:
```python
import functools

import jax
import jax.numpy as jnp
from jax import lax
from jax.experimental import pallas as pl
from jax.experimental.pallas import tpu as pltpu
from jax.sharding import PartitionSpec as P

TILE = 64
MESH = pl.DeviceIdType.MESH

LEVELS = ((9, 24, 24), (9, 26, 26), (10, 28, 28), (12, 34, 34), (16, 64, 64))


def place():
    row = lax.axis_index("row")
    col = lax.axis_index("col")
    core = col % 2
    z, y = row // 4, row % 4
    p = (1 - core) * y + core * z
    q = (1 - core) * z + core * y
    return row, col, col // 2, core, p, q


def row_at(core, p, q):
    return (p * 4 + q) * core + (q * 4 + p) * (1 - core)


def ring_places(here):
    away = [(g - here + 4) % 4 for g in range(4)]
    return [2 * (d == 1) + 3 * (d == 2) + 1 * (d == 3) for d in away]


def table_kernel(mask_a, mask_b, tab, level):
    row, col, x, core, p, q = place()

    def clear(t, _):
        for k in range(16):
            tab[t * 16 + k] = 0
        return 0

    lax.fori_loop(0, 12, clear, 0)

    def scan_a(a, carry):
        count, totals = carry[0], list(carry[1:])
        for cc in range(4):
            tab[count] = ((cc // 2) * 16 + a) * 2 + cc % 2
            count += mask_a[a, 4 * x + cc]
        for g in range(4):
            for cc in range(4):
                totals[g] += mask_a[a, 4 * g + cc]
        return (count, *totals)

    zero = jnp.int32(0)
    most_a = functools.reduce(jnp.maximum, lax.fori_loop(0, 16, scan_a, (zero,) * 5)[1:])

    def scan_row(c, count):
        tab[64 + count] = c
        return count + mask_b[row, c]

    lax.fori_loop(0, 16, scan_row, zero, unroll=True)

    def scan_b(g, carry):
        most_row, most_z, by_y = carry[0], carry[1], list(carry[2:])
        total = zero
        for k in range(4):
            count = zero
            for c in range(16):
                count += mask_b[4 * g + k, c]
            most_row = jnp.maximum(most_row, count)
            by_y[k] += count
            total += count
        return (most_row, jnp.maximum(most_z, total), *by_y)

    most_row, most_z, *by_y = lax.fori_loop(0, 4, scan_b, (zero,) * 6)
    most_b = functools.reduce(jnp.maximum, by_y, most_z)

    def scan_pool(k, count):
        rank = zero
        here = row_at(core, k, q)
        for c in range(16):
            tab[128 + count] = k * 16 + rank
            bit = mask_b[here, c]
            count += bit
            rank += bit
        return count

    lax.fori_loop(0, 4, scan_pool, zero)

    found = zero
    for c1, ca, cb in LEVELS[:-1]:
        found += ((most_row > c1) | (most_a > ca) | (most_b > cb)).astype(jnp.int32)
    level[0] = found


def tables(mask_amp, mask_int):
    smem = pl.BlockSpec(memory_space=pltpu.SMEM)
    return pl.pallas_call(
        table_kernel,
        out_shape=(jax.ShapeDtypeStruct((192,), jnp.int32), jax.ShapeDtypeStruct((1,), jnp.int32)),
        in_specs=[smem, smem],
        out_specs=(smem, smem),
    )(mask_amp, mask_int)


def comm_kernel(
    cap1, capa, capb, tab, mask_a, mask_b, amp, integ, out,
    recv_a, recv_b, grp_b1, ga0, ga1, ga2, ga3, gb0, gb1, gb2, gb3, dense_a, dense_b, acc, narrow,
    a1_send, a1_recv, b1_send, b1_recv, ring_send, ring_recv, sib_send, sib_recv, out_sem,
):
    grp_a, grp_b = (ga0, ga1, ga2, ga3), (gb0, gb1, gb2, gb3)
    row, col, x, core, p, q = place()
    sibling = (row, 2 * x + 1 - core)

    barrier = pltpu.get_barrier_semaphore()

    def signal(target):
        pl.semaphore_signal(barrier, inc=1, device_id=target, device_id_type=MESH)

    for d in range(1, 4):
        for cc in range(2):
            signal((row, 2 * ((x + d) % 4) + cc))
    signal(sibling)
    for d in range(1, 16):
        for cc in range(2):
            signal(((row + d) % 16, 2 * x + cc))
    pl.semaphore_wait(barrier, 37)

    def b1_copy(d):
        target = (col + d) % 8
        return pltpu.make_async_remote_copy(
            src_ref=integ.at[:, target], dst_ref=recv_b.at[col],
            send_sem=b1_send, recv_sem=b1_recv,
            device_id=(row, target), device_id_type=MESH,
        )

    for d in range(1, 8):
        b1_copy(d).start()
    pltpu.make_async_copy(integ.at[:, col], recv_b.at[col], b1_recv).start()

    def a1_copy(d, cc):
        target = (row + d) % 16
        return pltpu.make_async_remote_copy(
            src_ref=amp.at[target, pl.ds(2 * cc, 2)], dst_ref=recv_a.at[core * 16 + row],
            send_sem=a1_send, recv_sem=a1_recv,
            device_id=(target, 2 * x + cc), device_id_type=MESH,
        )

    for d in range(1, 16):
        for cc in range(2):
            a1_copy(d, cc).start()
    a1_copy(0, 1 - core).start()
    pltpu.make_async_copy(amp.at[row, pl.ds(2 * core, 2)], recv_a.at[core * 16 + row], a1_recv).start()

    for g in range(4):
        grp_a[g][:, capa] = jnp.zeros((2, TILE, 128), jnp.bfloat16)
        grp_b[g][capb] = jnp.zeros((2, TILE, 128), jnp.bfloat16)
    half = lax.broadcasted_iota(jnp.int32, (TILE, 128), 1) // TILE

    def mixed(first, second, parity):
        turned = pltpu.roll(second.astype(jnp.float32), TILE, 1)
        return jnp.where(half == parity, first.astype(jnp.float32), turned).astype(jnp.bfloat16)

    class Ring:
        def __init__(self, which, view, pos, cap, target_of, absolute=False):
            right, left, cut = (pos + 1) % 4, (pos + 3) % 4, cap // 2

            def copy(k, src, dst, to, s, e):
                if absolute:
                    src = dst = (pos + src) % 4
                return pltpu.make_async_remote_copy(
                    src_ref=view(src, s, e), dst_ref=view(dst, s, e), send_sem=ring_send.at[which, k],
                    recv_sem=ring_recv.at[which, k], device_id=target_of(to), device_id_type=MESH,
                )

            self.first_right = copy(0, 0, 3, right, 0, cut)
            self.first_left = copy(1, 0, 1, left, cut, cap)
            self.rest_right = copy(2, 0, 3, right, cut, cap)
            self.rest_left = copy(3, 0, 1, left, 0, cut)
            self.on_right = copy(4, 3, 2, right, 0, cut)
            self.on_left = copy(5, 1, 2, left, cut, cap)

        def start(self):
            self.first_right.start()
            self.first_left.start()
            self.rest_right.start()
            self.rest_left.start()

        def forward(self):
            self.first_right.wait_recv()
            self.on_right.start()
            self.first_left.wait_recv()
            self.on_left.start()

        def wait_opposite(self):
            self.on_right.wait_recv()
            self.on_left.wait_recv()

        def wait_sends(self):
            for c in (self.first_right, self.first_left, self.rest_right, self.rest_left,
                      self.on_right, self.on_left):
                c.wait_send()

    ring_b1 = Ring(0, lambda at, s, e: grp_b1.at[at, pl.ds(s, e - s)], p, cap1,
                   lambda to: (row_at(core, to, q), col), absolute=True)
    ring_b2 = Ring(1, lambda g, s, e: grp_b[g].at[pl.ds(s, e - s)], q, capb,
                   lambda to: (row_at(core, p, to), col))
    ring_a = Ring(2, lambda g, s, e: grp_a[g].at[core, pl.ds(s, e - s)], x, capa,
                  lambda to: (row, 2 * to + core))

    def sib_copy(g):
        ref = grp_a[g].at[core, pl.ds(0, capa)]
        return pltpu.make_async_remote_copy(
            src_ref=ref, dst_ref=ref, send_sem=sib_send.at[g], recv_sem=sib_recv.at[g],
            device_id=sibling, device_id_type=MESH,
        )

    def sib_wait(g):
        there = grp_a[g].at[1 - core, pl.ds(0, capa)]
        pltpu.make_async_copy(there, there, sib_recv.at[g]).wait()

    def expand_a(rel, pos):
        g = (x + rel) % 4

        def body(a, count):
            for cc in range(4):
                bit = mask_a[a, 4 * g + cc]
                slot = jnp.where(bit > 0, count, capa)
                count += bit
                for kp in range(2):
                    dense_a[pl.ds(a * TILE, TILE), pl.ds(pos * 1024 + (2 * cc + kp) * 128, 128)] = (
                        grp_a[rel][kp, slot]
                    )
            return count

        lax.fori_loop(0, 16, body, jnp.int32(0))

    def expand_b(rel, pos):
        g = (q + rel) % 4
        first = [pl.multiple_of(1024 * v, 1024) for v in ring_places(x)]

        def body(k, count):
            here = row_at(core, k, g)
            for c in range(16):
                bit = mask_b[here, c]
                slot = jnp.where(bit > 0, count, capb)
                count += bit
                for kp in range(2):
                    lanes = pl.ds(first[c // 4] + (2 * (c % 4) + kp) * 128, 128)
                    dense_b[pl.ds(pos * 256 + k * TILE, TILE), lanes] = grp_b[rel][slot, kp]
            return count

        lax.fori_loop(0, 4, body, jnp.int32(0))

    def by_rows(done, columns, depth):
        def body(t, _):
            rows = pl.ds(t * 512, 512)
            done(rows, lax.dot_general(
                dense_a[rows, pl.ds(*depth)], dense_b[pl.ds(*columns), pl.ds(*depth)],
                (((1,), (1,)), ((), ())), preferred_element_type=jnp.float32,
            ))
            return 0

        lax.fori_loop(0, 2, body, 0)

    def out_copy(rel, pos):
        return pltpu.make_async_copy(narrow.at[pos], out.at[(q + rel) % 4], out_sem.at[pos])

    pltpu.make_async_copy(recv_b, recv_b, b1_recv).wait()

    def pack_b(s, _):
        e = tab[64 + s]
        for kp in range(2):
            grp_b1[p, s, kp] = mixed(recv_b[e // 2, 2 * kp], recv_b[e // 2, 2 * kp + 1], e % 2)
        return 0

    lax.fori_loop(0, cap1, pack_b, 0)
    ring_b1.start()
    ring_b1.forward()

    pltpu.make_async_copy(recv_a, recv_a, a1_recv).wait()

    def pack_a(s, _):
        e = tab[s]
        grp_a[0][core, s] = mixed(recv_a[e // 2, 0], recv_a[e // 2, 1], e % 2)
        return 0

    lax.fori_loop(0, capa, pack_a, 0)
    ring_a.start()
    sib_copy(0).start()

    ring_b1.rest_right.wait_recv()
    ring_b1.rest_left.wait_recv()
    ring_b1.wait_opposite()

    def pack_b2(s, _):
        e = tab[128 + s]
        grp_b[0][s] = grp_b1[e // 16, e % 16]
        return 0

    lax.fori_loop(0, capb, pack_b2, 0)
    ring_b2.start()

    ring_a.forward()
    expand_b(0, 0)
    sib_wait(0)
    expand_a(0, 0)

    def put_own(rows, value):
        acc[rows, 0:256] = value

    by_rows(put_own, (0, 256), (0, 1024))

    ring_b2.forward()
    ring_a.rest_right.wait_recv()
    sib_copy(3).start()
    ring_a.rest_left.wait_recv()
    sib_copy(1).start()
    sib_wait(3)
    expand_a(3, 1)
    sib_wait(1)
    expand_a(1, 2)

    def add_own(rows, value):
        acc[rows, 0:256] += value

    by_rows(add_own, (0, 256), (1024, 2048))

    ring_b2.rest_right.wait_recv()
    expand_b(3, 1)
    ring_b2.rest_left.wait_recv()
    expand_b(1, 2)

    def put_sides(rows, value):
        acc[rows, 256:768] = value

    by_rows(put_sides, (256, 512), (0, 3072))

    ring_a.wait_opposite()
    sib_copy(2).start()
    sib_wait(2)
    expand_a(2, 3)

    def finish_three(rows, value):
        total = (acc[rows] + value).astype(jnp.bfloat16)
        for g in range(3):
            narrow[g, rows] = total[:, g * 256:(g + 1) * 256]

    by_rows(finish_three, (0, 768), (3072, 1024))
    for pos, rel in enumerate((0, 3, 1)):
        out_copy(rel, pos).start()

    ring_b2.wait_opposite()
    expand_b(2, 3)

    def finish_last(rows, value):
        narrow[3, rows] = value.astype(jnp.bfloat16)

    by_rows(finish_last, (768, 256), (0, 4096))
    out_copy(2, 3).start()

    for d in range(1, 8):
        b1_copy(d).wait_send()
    for d in range(1, 16):
        for cc in range(2):
            a1_copy(d, cc).wait_send()
    a1_copy(0, 1 - core).wait_send()
    for ring in (ring_b1, ring_b2, ring_a):
        ring.wait_sends()
    for g in range(4):
        sib_copy(g).wait_send()
    for pos, rel in enumerate((0, 3, 1, 2)):
        out_copy(rel, pos).wait()


def contract(level, tab, mask_amp, mask_int, amp, integ):
    cap1, capa, capb = LEVELS[level]
    bf16 = jnp.bfloat16
    dma = pltpu.SemaphoreType.DMA
    smem = pl.BlockSpec(memory_space=pltpu.SMEM)
    anywhere = pl.BlockSpec(memory_space=pl.ANY)
    return pl.pallas_call(
        functools.partial(comm_kernel, cap1, capa, capb),
        out_shape=jax.ShapeDtypeStruct((4, 1024, 256), bf16),
        in_specs=[smem, smem, smem, anywhere, anywhere],
        out_specs=anywhere,
        scratch_shapes=[
            pltpu.VMEM((32, 2, TILE, 128), bf16),
            pltpu.VMEM((8, 4, TILE, 128), bf16),
            pltpu.VMEM((4, cap1, 2, TILE, 128), bf16),
            *[pltpu.VMEM((2, capa + 1, TILE, 128), bf16)] * 4,
            *[pltpu.VMEM((capb + 1, 2, TILE, 128), bf16)] * 4,
            pltpu.VMEM((1024, 4096), bf16),
            pltpu.VMEM((1024, 4096), bf16),
            pltpu.VMEM((1024, 768), jnp.float32),
            pltpu.VMEM((4, 1024, 256), bf16),
            dma, dma, dma, dma,
            dma((3, 6)), dma((3, 6)), dma((4,)), dma((4,)), dma((4,)),
        ],
        compiler_params=pltpu.CompilerParams(
            collective_id=level + 1, has_side_effects=True, vmem_limit_bytes=60 << 20
        ),
    )(tab, mask_amp, mask_int, amp, integ)


def update_kernel(cycle, energy_a, energy_b, occ_i, occ_j, out):
    core = lax.axis_index("col") % 2
    rows = out.shape[2]
    down = jnp.transpose(jnp.broadcast_to(energy_a[...], (128, rows)))

    def emit(m, value):
        lanes = pl.ds(m * 128, 128)
        denominator = down + energy_b[:, lanes] - occ_i[0] - occ_j[0]
        out[0, 0, :, lanes] = (value.astype(jnp.float32) / denominator).astype(jnp.bfloat16)

    @pl.when(core == 0)
    def _():
        for m in range(8):
            emit(m, cycle[m // 2, :, pl.ds((m % 2) * 128, 128)])

    @pl.when(core == 1)
    def _():
        for m in range(8):
            k, g = m // 2, 2 * (m % 2)
            pair = [cycle[g + s, :, pl.ds((k // 2) * 128, 128)].astype(jnp.float32)
                    [:, (k % 2) * TILE:(k % 2 + 1) * TILE] for s in range(2)]
            emit(m, jnp.concatenate(pair, axis=1))


def update(cycle, virtual_energy, occupied_i, occupied_j):
    energies = virtual_energy.reshape(1, 1024)
    smem = pl.BlockSpec(memory_space=pltpu.SMEM)
    rows = 128
    return pl.pallas_call(
        update_kernel,
        grid=(1024 // rows,),
        out_shape=jax.ShapeDtypeStruct((1, 1, 1024, 1024), jnp.bfloat16),
        in_specs=[
            pl.BlockSpec((4, rows, 256), lambda t: (0, t, 0)),
            pl.BlockSpec((1, rows), lambda t: (0, t)),
            pl.BlockSpec((1, 1024), lambda t: (0, 0)),
            smem, smem,
        ],
        out_specs=pl.BlockSpec((1, 1, rows, 1024), lambda t: (0, 0, t, 0)),
    )(cycle, energies, energies, occupied_i, occupied_j)


def per_device(
    amplitudes, cycle_integrals, mask_amp, mask_int, occupied_i, occupied_j, virtual_energy
):
    tab, level = tables(mask_amp, mask_int)
    branches = [functools.partial(contract, k) for k in range(len(LEVELS))]
    cycle = lax.switch(level[0], branches, tab, mask_amp, mask_int, amplitudes, cycle_integrals)
    return update(cycle, virtual_energy, occupied_i, occupied_j)


def solution(mesh):
    in_specs = (
        P(None, None, "row", "col"),
        P(None, None, "row", "col"),
        P(),
        P(),
        P("row"),
        P("col"),
        P(),
    )
    out_specs = P("row", "col", None, None)
    return jax.shard_map(
        per_device, mesh=mesh, in_specs=in_specs, out_specs=out_specs, check_vma=False
    )
```

time: 902 us -> 68.9 us (0.08)
  waiting for transfers between devices: 436 us -> 0 us
  blocking collectives: 369 us -> 0 us
  Pallas kernels: 0 us -> 66.1 us
  local copies, waits for them, and re-layouts: 35.8 us -> 0 us
  matrix products: 18.9 us -> 0 us
  other arithmetic: 17.8 us -> 0 us
  between operations: 14.7 us -> 1.96 us
  starting transfers between devices: 9.05 us -> 0 us
    all_to_all x1 -> x0, blocking collectives: 369 us -> none  [per_device(): lax.all_to_all(partial_value[None], 'row', split_axis=1, concat_axis=3, t...]
    all_to_all x1 -> x0, waiting for transfers between devices: 362 us -> none  [per_device(): lax.all_to_all(lax.all_to_all(partial_value[None], 'row', split_axis=1, c...]
    all_gather x1 -> x0, waiting for transfers between devices: 74.1 us -> none  [per_device(): lax.all_gather(int_masked, 'row', axis=2, tiled=True)]
    pallas_call x0 -> x3, Pallas kernels: none -> 66.1 us  [the longest x1 57.9 us: contract(): pl.pallas_call(functools.partial(comm_kernel, cap1, capa, capb), out_shap...]
    all_to_all x1 -> x0, local copies, waits for them, and re-layouts: 23.3 us -> none  [per_device(): lax.all_to_all(partial_value[None], 'row', split_axis=1, concat_axis=3, t...]
    dot_general x1 -> x0, matrix products: 18.9 us -> none  [per_device(): jnp.einsum('ikac,kjbc->ijab', amp_masked, lax.all_gather(int_masked, 'row...]
    reduce_sum x1 -> x0, other arithmetic: 12.9 us -> none  [per_device(): cycle = jnp.sum(exchanged, axis=0).astype(jnp.bfloat16)]
    broadcast_in_dim x3 -> x0, local copies, waits for them, and re-layouts: 12.2 us -> none  [the longest x1 12.1 us: per_device(): partial_value[None]]
  transfers between devices with their start and end apart: 2 -> 0, of which waited for: 2 -> 0; matrix products, arithmetic and copies ran while one was open for 0% -> 0% of each run, Pallas kernels for 0% -> 0%
where the time goes in v2:
time: 68.9 us; the launch traced here: 68.5 us
  Pallas kernels  66.1 us (96%)
  between operations  1.96 us (3%)
    pallas_call x1, Pallas kernels, contract(): pl.pallas_call(functools.partial(comm_kernel, cap1, capa, capb), out_shap...  57.9 us
    pallas_call x1, Pallas kernels, update(): pl.pallas_call(update_kernel, grid=(1024 // rows,), out_shape=jax.ShapeDt...  5.54 us
    pallas_call x1, Pallas kernels, tables(): pl.pallas_call(table_kernel, out_shape=(jax.ShapeDtypeStruct((192,), jnp....  2.7 us

profile of v2, /device:TPU:1, one launch (start us, length us, event | category | flops | bytes accessed | tf_op | source)
XLA Modules:
  0.0 68.5 jit_solution(6641841220993972940)
XLA Ops:
  0.0 2.7 %shard_map.73 = (s32[192]{0:T(256)S(1)}, s32[1]{0:T(128)}) custom-call(s32[16,16]{1,0:T(8,128)} %mask_a.1, s32[16,16]{1,0:T(8,128)} %mask_b.1), custom_call_target="tpu_custom_call" | custom-call | tf_op jit(solution)/shard_map/pallas_call | solution.py:99
  3.4 58.3 %conditional.1 = (bf16[4,1024,256]{2,1,0:T(8,128)(2,1)S(1)}) conditional(s32[]{:T(128)} %bitcast, (s32[192]{0:T(256)S(1)}, s32[16,16]{1,0:T(8,128)}, s32[16,16]{1,0:T(8,128)}, bf16[16,4,64,128]{3,2,1,0:T(8,128)(2,1)}, bf16[4,8,64,128]{3,2,1,0:T(8,128)(2,1)}) %tuple.20, (s32[192]{0:T(256)S(1)}, s32[16,16]{1,0:T(8,128)}, ...), branch_computations={%region_0.0_spmd, %region_1.0_spmd, %region_2.0_spmd, %region_3.0_... | conditional | bytes 8 | solution.py:454
  3.6 57.9 %branch_2_fun.1 = bf16[4,1024,256]{2,1,0:T(8,128)(2,1)S(1)} custom-call(s32[192]{0:T(256)S(1)} %get-tuple-element.71.tab, s32[16,16]{1,0:T(8,128)} %get-tuple-element.72.mask_a, s32[16,16]{1,0:T(8,128)} %get-tuple-element.73.mask_b, bf16[16,4,64,128]{3,2,1,0:T(8,128)(2,1)} %get-tuple-element.74.amp, bf16[4,8,64,128]{3,2,1,0:T(8,128)(2,1)} %get-tuple-element.75.integ), custom_call_target="tpu_custom_call" | custom-call | tf_op jit(solution)/shard_map/cond/branch_2_fun/pallas_call | solution.py:383
  63.0 5.5 %shard_map.74 = bf16[1,1,1024,1024]{3,2,1,0:T(8,128)(2,1)} custom-call(bf16[4,1024,256]{2,1,0:T(8,128)(2,1)S(1)} %get-tuple-element.90.cycle, f32[1,1024]{1,0:T(1,128)} %bitcast.2, f32[1,1024]{1,0:T(1,128)} %bitcast.3, f32[1]{0:T(128)S(6)} %copy.13.occ_i, f32[1]{0:T(128)S(6)} %copy.14.occ_j), custom_call_target="tpu_custom_call" | custom-call | tf_op jit(solution)/shard_map/pallas_call | solution.py:435

commit v3 on v2

v3 whole, which is shorter than its diff:
```python
import functools

import jax
import jax.numpy as jnp
from jax import lax
from jax.experimental import pallas as pl
from jax.experimental.pallas import tpu as pltpu
from jax.sharding import PartitionSpec as P

TILE = 64
HALF = 32
MESH = pl.DeviceIdType.MESH

LEVELS = ((9, 24, 24), (10, 28, 28), (12, 34, 34), (16, 64, 64))


def place():
    row = lax.axis_index("row")
    col = lax.axis_index("col")
    core = col % 2
    z, y = row // 4, row % 4
    p = (1 - core) * y + core * z
    q = (1 - core) * z + core * y
    return row, col, col // 2, core, p, q


def row_at(core, p, q):
    return (p * 4 + q) * core + (q * 4 + p) * (1 - core)


def ring_places(here):
    away = [(g - here + 4) % 4 for g in range(4)]
    return [2 * (d == 1) + 3 * (d == 2) + 1 * (d == 3) for d in away]


def table_kernel(mask_a, mask_b, tab, level):
    row, col, x, core, p, q = place()

    def clear(t, _):
        for k in range(16):
            tab[t * 16 + k] = 0
        return 0

    lax.fori_loop(0, 12, clear, 0)

    def scan_a(a, carry):
        count, totals = carry[0], list(carry[1:])
        for cc in range(4):
            tab[count] = ((cc // 2) * 16 + a) * 2 + cc % 2
            count += mask_a[a, 4 * x + cc]
        for g in range(4):
            for cc in range(4):
                totals[g] += mask_a[a, 4 * g + cc]
        return (count, *totals)

    zero = jnp.int32(0)
    most_a = functools.reduce(jnp.maximum, lax.fori_loop(0, 16, scan_a, (zero,) * 5)[1:])

    def scan_row(c, count):
        tab[64 + count] = c
        return count + mask_b[row, c]

    lax.fori_loop(0, 16, scan_row, zero, unroll=True)

    def scan_b(g, carry):
        most_row, most_z, by_y = carry[0], carry[1], list(carry[2:])
        total = zero
        for k in range(4):
            count = zero
            for c in range(16):
                count += mask_b[4 * g + k, c]
            most_row = jnp.maximum(most_row, count)
            by_y[k] += count
            total += count
        return (most_row, jnp.maximum(most_z, total), *by_y)

    most_row, most_z, *by_y = lax.fori_loop(0, 4, scan_b, (zero,) * 6)
    most_b = functools.reduce(jnp.maximum, by_y, most_z)

    def scan_pool(k, count):
        rank = zero
        here = row_at(core, k, q)
        for c in range(16):
            tab[128 + count] = k * 16 + rank
            bit = mask_b[here, c]
            count += bit
            rank += bit
        return count

    lax.fori_loop(0, 4, scan_pool, zero)

    found = zero
    for c1, ca, cb in LEVELS[:-1]:
        found += ((most_row > c1) | (most_a > ca) | (most_b > cb)).astype(jnp.int32)
    level[0] = found


def tables(mask_amp, mask_int):
    smem = pl.BlockSpec(memory_space=pltpu.SMEM)
    return pl.pallas_call(
        table_kernel,
        out_shape=(jax.ShapeDtypeStruct((192,), jnp.int32), jax.ShapeDtypeStruct((1,), jnp.int32)),
        in_specs=[smem, smem],
        out_specs=(smem, smem),
    )(mask_amp, mask_int)


def comm_kernel(
    cap1, capa, capb, tab_in, mask_a_in, mask_b_in, occ_i_in, occ_j_in, energy_in, amp, integ, out,
    tab, mask_a, mask_b, occ_i, occ_j, energy,
    ra0, ra1, rb0, rb1, b10, b11, ga0, ga1, ga2, ga3, gb0, gb1, gb2, gb3, gb4, gb5, gb6, gb7,
    dense_a, dense_b, acc, narrow, inverse, staged, small_sem,
    a1_send, a1_recv, b1_send, b1_recv, ring_send, ring_recv, sib_send, sib_recv, out_sem,
):
    recv_a, recv_b, grp_b1 = (ra0, ra1), (rb0, rb1), (b10, b11)
    grp_a, grp_b = (ga0, ga1, ga2, ga3), ((gb0, gb1), (gb2, gb3), (gb4, gb5), (gb6, gb7))
    row, col, x, core, p, q = place()
    sibling = (row, 2 * x + 1 - core)

    barrier = pltpu.get_barrier_semaphore()

    def signal(target):
        pl.semaphore_signal(barrier, inc=1, device_id=target, device_id_type=MESH)

    for d in range(1, 16):
        for cc in range(2):
            signal(((row + d) % 16, 2 * x + cc))
    for d in range(1, 4):
        for cc in range(2):
            signal((row, 2 * ((x + d) % 4) + cc))
    signal(sibling)
    small = [
        pltpu.make_async_copy(src, dst, small_sem.at[n]) for n, (src, dst) in enumerate((
            (tab_in, tab), (mask_a_in, mask_a), (mask_b_in, mask_b),
            (occ_i_in, occ_i), (occ_j_in, occ_j), (energy_in, energy),
        ))
    ]
    for copy in small:
        copy.start()
    pl.semaphore_wait(barrier, 37)

    def b1_copy(d, h):
        target = (col + d) % 8
        return pltpu.make_async_remote_copy(
            src_ref=integ.at[pl.ds(2 * h, 2), target], dst_ref=recv_b[h].at[col],
            send_sem=b1_send.at[h], recv_sem=b1_recv.at[h],
            device_id=(row, target), device_id_type=MESH,
        )

    def a1_copy(d, cc, h):
        target = (row + d) % 16
        return pltpu.make_async_remote_copy(
            src_ref=amp.at[target, pl.ds(2 * cc, 2), pl.ds(h * HALF, HALF)],
            dst_ref=recv_a[h].at[core * 16 + row],
            send_sem=a1_send.at[h], recv_sem=a1_recv.at[h],
            device_id=(target, 2 * x + cc), device_id_type=MESH,
        )

    a1_targets = [(d, cc) for d in range(1, 16) for cc in range(2)]
    for h in range(2):
        for d in range(1, 8):
            b1_copy(d, h).start()
        pltpu.make_async_copy(
            integ.at[pl.ds(2 * h, 2), col], recv_b[h].at[col], b1_recv.at[h]
        ).start()
        for d, cc in a1_targets:
            a1_copy(d, cc, h).start()
        a1_copy(0, 1 - core, h).start()
        pltpu.make_async_copy(
            amp.at[row, pl.ds(2 * core, 2), pl.ds(h * HALF, HALF)],
            recv_a[h].at[core * 16 + row], a1_recv.at[h],
        ).start()

    for g in range(4):
        grp_a[g][:, :, capa] = jnp.zeros((2, 2, HALF, 128), jnp.bfloat16)
        for h in range(2):
            grp_b[g][h][capb] = jnp.zeros((TILE, 128), jnp.bfloat16)

    def mixed(first, second, parity):
        side = lax.broadcasted_iota(jnp.int32, first.shape, 1) // TILE
        turned = pltpu.roll(second.astype(jnp.float32), TILE, 1)
        return jnp.where(side == parity, first.astype(jnp.float32), turned).astype(jnp.bfloat16)

    class Ring:
        def __init__(self, which, view, pos, cap, target_of, absolute=False):
            right, left, cut = (pos + 1) % 4, (pos + 3) % 4, cap // 2

            def copy(h, k, src, dst, to, s, e):
                if absolute:
                    src = dst = (pos + src) % 4
                return pltpu.make_async_remote_copy(
                    src_ref=view(h, src, s, e), dst_ref=view(h, dst, s, e),
                    send_sem=ring_send.at[which, h, k], recv_sem=ring_recv.at[which, h, k],
                    device_id=target_of(to), device_id_type=MESH,
                )

            self.copies = [(
                copy(h, 0, 0, 3, right, 0, cap), copy(h, 1, 0, 1, left, 0, cap),
                copy(h, 2, 3, 2, right, 0, cut), copy(h, 3, 1, 2, left, cut, cap),
            ) for h in range(2)]

        def start(self, h):
            self.copies[h][0].start()
            self.copies[h][1].start()

        def forward(self, h):
            for k in range(2):
                self.copies[h][k].wait_recv()
                self.copies[h][2 + k].start()

        def wait_opposite(self, h):
            self.copies[h][2].wait_recv()
            self.copies[h][3].wait_recv()

        def wait_sends(self):
            for h in range(2):
                for c in self.copies[h]:
                    c.wait_send()

    ring_b1 = Ring(0, lambda h, at, s, e: grp_b1[h].at[at, pl.ds(s, e - s)], p, cap1,
                   lambda to: (row_at(core, to, q), col), absolute=True)
    ring_b2 = Ring(1, lambda h, g, s, e: grp_b[g][h].at[pl.ds(s, e - s)], q, capb,
                   lambda to: (row_at(core, p, to), col))
    ring_a = Ring(2, lambda h, g, s, e: grp_a[g].at[core, h, pl.ds(s, e - s)], x, capa,
                  lambda to: (row, 2 * to + core))

    def sib_copy(g, h):
        ref = grp_a[g].at[core, h, pl.ds(0, capa)]
        return pltpu.make_async_remote_copy(
            src_ref=ref, dst_ref=ref, send_sem=sib_send.at[g, h], recv_sem=sib_recv.at[g, h],
            device_id=sibling, device_id_type=MESH,
        )

    def sib_wait(g):
        for h in range(2):
            there = grp_a[g].at[1 - core, h, pl.ds(0, capa)]
            pltpu.make_async_copy(there, there, sib_recv.at[g, h]).wait()

    def expand_a(rel, pos):
        g = (x + rel) % 4

        def body(a, count):
            for cc in range(4):
                bit = mask_a[a, 4 * g + cc]
                slot = jnp.where(bit > 0, count, capa)
                count += bit
                for kp in range(2):
                    lanes = pl.ds(kp * 2048 + pos * 512 + cc * 128, 128)
                    for h in range(2):
                        dense_a[pl.ds(a * TILE + h * HALF, HALF), lanes] = grp_a[rel][kp, h, slot]
            return count

        lax.fori_loop(0, 16, body, jnp.int32(0))

    def expand_b(rel, pos, kp):
        g = (q + rel) % 4
        first = [pl.multiple_of(512 * v, 512) for v in ring_places(x)]

        def body(k, count):
            here = row_at(core, k, g)
            for c in range(16):
                bit = mask_b[here, c]
                slot = jnp.where(bit > 0, count, capb)
                count += bit
                lanes = pl.ds(kp * 2048 + first[c // 4] + (c % 4) * 128, 128)
                dense_b[pl.ds(pos * 256 + k * TILE, TILE), lanes] = grp_b[rel][kp][slot]
            return count

        lax.fori_loop(0, 4, body, jnp.int32(0))

    def by_rows(done, columns, pairs, places):
        def body(t, _):
            rows = pl.ds(t * 512, 512)
            total = None
            for kp in pairs:
                depth = pl.ds(kp * 2048 + places[0] * 512, places[1] * 512)
                part = lax.dot_general(
                    dense_a[rows, depth], dense_b[pl.ds(*columns), depth],
                    (((1,), (1,)), ((), ())), preferred_element_type=jnp.float32,
                )
                total = part if total is None else total + part
            done(rows, pl.ds(*columns), total)
            return 0

        lax.fori_loop(0, 2, body, 0)

    def put(rows, lanes, value):
        acc[rows, lanes] = value

    def add(rows, lanes, value):
        acc[rows, lanes] += value

    def pack_b(h):
        def body(s, _):
            e = tab[64 + s]
            grp_b1[h][p, s] = mixed(recv_b[h][e // 2, 0], recv_b[h][e // 2, 1], e % 2)
            return 0

        lax.fori_loop(0, cap1, body, 0)

    def pack_a(h):
        def body(s, _):
            e = tab[s]
            grp_a[0][core, h, s] = mixed(recv_a[h][e // 2, 0], recv_a[h][e // 2, 1], e % 2)
            return 0

        lax.fori_loop(0, capa, body, 0)

    def pool_b(h):
        def body(s, _):
            e = tab[128 + s]
            grp_b[0][h][s] = grp_b1[h][e // 16, e % 16]
            return 0

        lax.fori_loop(0, capb, body, 0)

    def invert(t, _):
        rows = pl.ds(t * 128, 128)
        down = jnp.transpose(jnp.broadcast_to(energy[:, rows], (128, 128)))
        for m in range(8):
            lanes = pl.ds(m * 128, 128)
            inverse[rows, lanes] = 1.0 / (down + energy[:, lanes] - occ_i[0] - occ_j[0])
        return 0

    def emit(rows, m, value):
        lanes = pl.ds(pl.multiple_of(m * 128, 128), 128)
        staged[rows, lanes] = (value * inverse[rows, lanes]).astype(jnp.bfloat16)

    def out_copy(m):
        lanes = pl.ds(pl.multiple_of(m * 128, 128), 128)
        return pltpu.make_async_copy(staged.at[:, lanes], out.at[:, lanes], out_sem.at[m])

    def finish_group(g):
        def body(t, _):
            rows = pl.ds(t * 128, 128)
            for s in range(2):
                emit(rows, 2 * g + s, narrow[g, rows, pl.ds(s * 128, 128)].astype(jnp.float32))
            return 0

        lax.fori_loop(0, 8, body, 0)
        for s in range(2):
            out_copy(2 * g + s).start()

    lower = lax.broadcasted_iota(jnp.int32, (128, 128), 1) < TILE

    def finish_pair(h):
        def body(t, _):
            rows = pl.ds(t * 128, 128)
            for k in range(4):
                one, two = [
                    narrow[2 * h + s, rows, pl.ds((k // 2) * 128, 128)].astype(jnp.float32) for s in range(2)
                ]
                if k % 2 == 0:
                    two = pltpu.roll(two, TILE, 1)
                else:
                    one = pltpu.roll(one, TILE, 1)
                emit(rows, 2 * k + h, jnp.where(lower, one, two))
            return 0

        lax.fori_loop(0, 8, body, 0)
        for k in range(4):
            out_copy(2 * k + h).start()

    for copy in small:
        copy.wait()
    lax.fori_loop(0, 8, invert, 0)

    for h in range(2):
        pltpu.make_async_copy(recv_b[h], recv_b[h], b1_recv.at[h]).wait()
        pack_b(h)
        ring_b1.start(h)

    for h in range(2):
        pltpu.make_async_copy(recv_a[h], recv_a[h], a1_recv.at[h]).wait()
        pack_a(h)
        ring_a.start(h)
        sib_copy(0, h).start()
        ring_b1.forward(h)

    for h in range(2):
        ring_b1.wait_opposite(h)
        pool_b(h)
        ring_b2.start(h)
        ring_a.forward(h)
        sib_copy(3, h).start()
        sib_copy(1, h).start()

    for kp in range(2):
        expand_b(0, 0, kp)
    sib_wait(0)
    expand_a(0, 0)
    by_rows(put, (0, 256), (0, 1), (0, 1))

    ring_b2.forward(0)
    sib_wait(3)
    expand_a(3, 1)
    sib_wait(1)
    expand_a(1, 2)
    by_rows(add, (0, 256), (0, 1), (1, 2))
    expand_b(3, 1, 0)
    expand_b(1, 2, 0)
    by_rows(put, (256, 512), (0,), (0, 3))

    ring_b2.forward(1)
    for h in range(2):
        ring_a.wait_opposite(h)
        sib_copy(2, h).start()
    expand_b(3, 1, 1)
    expand_b(1, 2, 1)
    by_rows(add, (256, 512), (1,), (0, 3))

    sib_wait(2)
    expand_a(2, 3)

    def finish_three(rows, lanes, value):
        total = (acc[rows, lanes] + value).astype(jnp.bfloat16)
        for pos, rel in enumerate((0, 3, 1)):
            narrow[(q + rel) % 4, rows] = total[:, pos * 256:(pos + 1) * 256]

    by_rows(finish_three, (0, 768), (0, 1), (3, 1))

    opposite = (q + 2) % 4

    ring_b2.wait_opposite(0)
    expand_b(2, 3, 0)
    by_rows(put, (768, 256), (0,), (0, 4))

    @pl.when(core == 0)
    def _():
        for rel in (0, 3, 1):
            finish_group((q + rel) % 4)

    @pl.when(core == 1)
    def _():
        finish_pair(1 - opposite // 2)

    ring_b2.wait_opposite(1)
    expand_b(2, 3, 1)

    def finish_last(rows, lanes, value):
        narrow[opposite, rows] = (acc[rows, lanes] + value).astype(jnp.bfloat16)

    by_rows(finish_last, (768, 256), (1,), (0, 4))

    @pl.when(core == 0)
    def _():
        finish_group(opposite)

    @pl.when(core == 1)
    def _():
        finish_pair(opposite // 2)

    for h in range(2):
        for d in range(1, 8):
            b1_copy(d, h).wait_send()
        for d, cc in a1_targets:
            a1_copy(d, cc, h).wait_send()
        a1_copy(0, 1 - core, h).wait_send()
        for g in range(4):
            sib_copy(g, h).wait_send()
    for ring in (ring_b1, ring_b2, ring_a):
        ring.wait_sends()
    for m in range(8):
        out_copy(m).wait()


def contract(level, tab, mask_amp, mask_int, occ_i, occ_j, energy, amp, integ):
    cap1, capa, capb = LEVELS[level]
    bf16 = jnp.bfloat16
    dma = pltpu.SemaphoreType.DMA
    anywhere = pl.BlockSpec(memory_space=pl.ANY)
    return pl.pallas_call(
        functools.partial(comm_kernel, cap1, capa, capb),
        out_shape=jax.ShapeDtypeStruct((1024, 1024), bf16),
        in_specs=[anywhere] * 8,
        out_specs=anywhere,
        scratch_shapes=[
            pltpu.SMEM((192,), jnp.int32),
            pltpu.SMEM((16, 16), jnp.int32),
            pltpu.SMEM((16, 16), jnp.int32),
            pltpu.SMEM((1,), jnp.float32),
            pltpu.SMEM((1,), jnp.float32),
            pltpu.VMEM((1, 1024), jnp.float32),
            *[pltpu.VMEM((32, 2, HALF, 128), bf16)] * 2,
            *[pltpu.VMEM((8, 2, TILE, 128), bf16)] * 2,
            *[pltpu.VMEM((4, cap1, TILE, 128), bf16)] * 2,
            *[pltpu.VMEM((2, 2, capa + 1, HALF, 128), bf16)] * 4,
            *[pltpu.VMEM((capb + 1, TILE, 128), bf16)] * 8,
            pltpu.VMEM((1024, 4096), bf16),
            pltpu.VMEM((1024, 4096), bf16),
            pltpu.VMEM((1024, 1024), jnp.float32),
            pltpu.VMEM((4, 1024, 256), bf16),
            pltpu.VMEM((1024, 1024), jnp.float32),
            pltpu.VMEM((1024, 1024), bf16),
            dma((6,)),
            dma((2,)), dma((2,)), dma((2,)), dma((2,)),
            dma((3, 2, 4)), dma((3, 2, 4)), dma((4, 2)), dma((4, 2)), dma((8,)),
        ],
        compiler_params=pltpu.CompilerParams(
            collective_id=level + 1, has_side_effects=True, vmem_limit_bytes=60 << 20
        ),
    )(tab, mask_amp, mask_int, occ_i, occ_j, energy, amp, integ)


def per_device(
    amplitudes, cycle_integrals, mask_amp, mask_int, occupied_i, occupied_j, virtual_energy
):
    tab, level = tables(mask_amp, mask_int)
    branches = [functools.partial(contract, k) for k in range(len(LEVELS))]
    update = lax.switch(
        level[0], branches, tab, mask_amp, mask_int, occupied_i, occupied_j,
        virtual_energy.reshape(1, -1), amplitudes, cycle_integrals,
    )
    return update[None, None]


def solution(mesh):
    in_specs = (
        P(None, None, "row", "col"),
        P(None, None, "row", "col"),
        P(),
        P(),
        P("row"),
        P("col"),
        P(),
    )
    out_specs = P("row", "col", None, None)
    return jax.shard_map(
        per_device, mesh=mesh, in_specs=in_specs, out_specs=out_specs, check_vma=False
    )
```

time: 68.9 us -> 60.9 us (0.88)
  Pallas kernels: 66.1 us -> 58 us
  local copies, waits for them, and re-layouts: 0 us -> 1.32 us
  between operations: 1.96 us -> 0.67 us
    pallas_call x1 -> x0, Pallas kernels: 5.54 us -> none  [update(): pl.pallas_call(update_kernel, grid=(1024 // rows,), out_shape=jax.ShapeDt...]
    pallas_call x1, Pallas kernels: 57.9 us -> 55.3 us  [contract(): pl.pallas_call(functools.partial(comm_kernel, cap1, capa, capb), out_shap...]
    unnamed x0 -> x1, local copies, waits for them, and re-layouts: none -> 1.32 us
where the time goes in v3:
time: 60.9 us; the launch traced here: 60.7 us
  Pallas kernels  58 us (95%)
  local copies, waits for them, and re-layouts  1.32 us (2%)
  loops' own time  0.74 us (1%)
  between operations  0.67 us (1%)
    pallas_call x1, Pallas kernels, contract(): pl.pallas_call(functools.partial(comm_kernel, cap1, capa, capb), out_shap...  55.3 us
    pallas_call x1, Pallas kernels, tables(): pl.pallas_call(table_kernel, out_shape=(jax.ShapeDtypeStruct((192,), jnp....  2.7 us
    unnamed x1, local copies, waits for them, and re-layouts  1.32 us

profile of v3, /device:TPU:1, one launch (start us, length us, event | category | flops | bytes accessed | tf_op | source)
XLA Modules:
  0.0 60.7 jit_solution(10496110434850291786)
XLA Ops:
  0.0 2.7 %shard_map.77 = (s32[192]{0:T(256)S(1)}, s32[1]{0:T(128)}) custom-call(s32[16,16]{1,0:T(8,128)} %mask_a.1, s32[16,16]{1,0:T(8,128)} %mask_b.1), custom_call_target="tpu_custom_call" | custom-call | tf_op jit(solution)/shard_map/pallas_call | solution.py:100
  3.4 56.1 %conditional.1 = (bf16[1,1,1024,1024]{3,2,1,0:T(8,128)(2,1)S(1)}) conditional(s32[]{:T(128)} %bitcast.4, (s32[192]{0:T(256)S(1)}, s32[16,16]{1,0:T(8,128)}, s32[16,16]{1,0:T(8,128)}, f32[1]{0:T(128)}, f32[1]{0:T(128)}, /*index=5*/f32[1,1024]{1,0:T(1,128)}, bf16[16,4,64,128]{3,2,1,0:T(8,128)(2,1)}, ...), branch_computations={%region_0.0_spmd, %region_1.0_spmd, %region_2.0_spmd, %region_3.0_... | conditional | bytes 8 | solution.py:510
  3.6 55.3 %branch_1_fun.1 = bf16[1024,1024]{1,0:T(8,128)(2,1)S(1)} custom-call(s32[192]{0:T(256)S(1)} %get-tuple-element.83.tab_in, s32[16,16]{1,0:T(8,128)} %get-tuple-element.84.mask_a_in, s32[16,16]{1,0:T(8,128)} %get-tuple-element.85.mask_b_in, f32[1]{0:T(128)} %get-tuple-element.86.occ_i_in, f32[1]{0:T(128)} %get-tuple-element.87.occ_j_in, ...), custom_call_target="tpu_custom_call" | custom-call | tf_op jit(solution)/shard_map/cond/branch_1_fun/pallas_call | solution.py:472
  59.4 1.3 %copy.17 = bf16[1,1,1024,1024]{3,2,1,0:T(8,128)(2,1)} copy(bf16[1,1,1024,1024]{3,2,1,0:T(8,128)(2,1)S(1)} %get-tuple-element.111) | data formatting | bytes 4194304

commit v4 on v3

--- a/solution.py
+++ b/solution.py
@@ -11,7 +11,7 @@
 HALF = 32
 MESH = pl.DeviceIdType.MESH
 
-LEVELS = ((9, 24, 24), (10, 28, 28), (12, 34, 34), (16, 64, 64))
+LEVELS = ((9, 26, 24), (10, 28, 26), (12, 34, 31), (16, 64, 64))
 
 
 def place():
@@ -26,11 +26,6 @@
 
 def row_at(core, p, q):
     return (p * 4 + q) * core + (q * 4 + p) * (1 - core)
-
-
-def ring_places(here):
-    away = [(g - here + 4) % 4 for g in range(4)]
-    return [2 * (d == 1) + 3 * (d == 2) + 1 * (d == 3) for d in away]
 
 
 def table_kernel(mask_a, mask_b, tab, level):
@@ -107,9 +102,9 @@
 
 def comm_kernel(
     cap1, capa, capb, tab_in, mask_a_in, mask_b_in, occ_i_in, occ_j_in, energy_in, amp, integ, out,
-    tab, mask_a, mask_b, occ_i, occ_j, energy,
+    tab, mask_a, mask_b, occ_i, occ_j, energy, slots,
     ra0, ra1, rb0, rb1, b10, b11, ga0, ga1, ga2, ga3, gb0, gb1, gb2, gb3, gb4, gb5, gb6, gb7,
-    dense_a, dense_b, acc, narrow, inverse, staged, small_sem,
+    acc, narrow, inverse, staged, small_sem,
     a1_send, a1_recv, b1_send, b1_recv, ring_send, ring_recv, sib_send, sib_recv, out_sem,
 ):
     recv_a, recv_b, grp_b1 = (ra0, ra1), (rb0, rb1), (b10, b11)
@@ -236,46 +231,62 @@
             there = grp_a[g].at[1 - core, h, pl.ds(0, capa)]
             pltpu.make_async_copy(there, there, sib_recv.at[g, h]).wait()
 
-    def expand_a(rel, pos):
-        g = (x + rel) % 4
-
-        def body(a, count):
+    def find_slots(rel):
+        ga, gb = (x + rel) % 4, (q + rel) % 4
+
+        def amplitudes(a, count):
             for cc in range(4):
-                bit = mask_a[a, 4 * g + cc]
-                slot = jnp.where(bit > 0, count, capa)
+                bit = mask_a[a, 4 * ga + cc]
+                slots[rel * 64 + a * 4 + cc] = jnp.where(bit > 0, count, capa)
                 count += bit
-                for kp in range(2):
-                    lanes = pl.ds(kp * 2048 + pos * 512 + cc * 128, 128)
-                    for h in range(2):
-                        dense_a[pl.ds(a * TILE + h * HALF, HALF), lanes] = grp_a[rel][kp, h, slot]
             return count
 
-        lax.fori_loop(0, 16, body, jnp.int32(0))
-
-    def expand_b(rel, pos, kp):
-        g = (q + rel) % 4
-        first = [pl.multiple_of(512 * v, 512) for v in ring_places(x)]
-
-        def body(k, count):
-            here = row_at(core, k, g)
+        def integrals(k, count):
+            here = row_at(core, k, gb)
             for c in range(16):
                 bit = mask_b[here, c]
-                slot = jnp.where(bit > 0, count, capb)
+                slots[256 + rel * 64 + k * 16 + c] = jnp.where(bit > 0, count, capb)
                 count += bit
-                lanes = pl.ds(kp * 2048 + first[c // 4] + (c % 4) * 128, 128)
-                dense_b[pl.ds(pos * 256 + k * TILE, TILE), lanes] = grp_b[rel][kp][slot]
             return count
 
-        lax.fori_loop(0, 4, body, jnp.int32(0))
+        lax.fori_loop(0, 16, amplitudes, jnp.int32(0))
+        lax.fori_loop(0, 4, integrals, jnp.int32(0))
+
+    by_place = (0, 3, 1, 2)
+
+    def packed_rows(rel, kp, places):
+        lines = []
+        for k in range(4):
+            tiles = []
+            for place_a in range(places[0], places[0] + places[1]):
+                group = (x + by_place[place_a]) % 4
+                for cc in range(4):
+                    tiles.append(grp_b[rel][kp][slots[256 + rel * 64 + k * 16 + 4 * group + cc]])
+            lines.append(jnp.concatenate(tiles, axis=1))
+        return lines
+
+    def packed_tall(t, kp, places):
+        lines = []
+        for a in range(8):
+            for h in range(2):
+                tiles = []
+                for place_a in range(places[0], places[0] + places[1]):
+                    rel = by_place[place_a]
+                    for cc in range(4):
+                        tiles.append(grp_a[rel][kp, h, slots[rel * 64 + (t * 8 + a) * 4 + cc]])
+                lines.append(jnp.concatenate(tiles, axis=1))
+        return jnp.concatenate(lines, axis=0)
 
     def by_rows(done, columns, pairs, places):
         def body(t, _):
             rows = pl.ds(t * 512, 512)
             total = None
             for kp in pairs:
-                depth = pl.ds(kp * 2048 + places[0] * 512, places[1] * 512)
+                lines = []
+                for place_b in range(columns[0] // 256, (columns[0] + columns[1]) // 256):
+                    lines += packed_rows(by_place[place_b], kp, places)
                 part = lax.dot_general(
-                    dense_a[rows, depth], dense_b[pl.ds(*columns), depth],
+                    packed_tall(t, kp, places), jnp.concatenate(lines, axis=0),
                     (((1,), (1,)), ((), ())), preferred_element_type=jnp.float32,
                 )
                 total = part if total is None else total + part
@@ -363,6 +374,8 @@
 
     for copy in small:
         copy.wait()
+    for rel in range(4):
+        find_slots(rel)
     lax.fori_loop(0, 8, invert, 0)
 
     for h in range(2):
@@ -385,32 +398,22 @@
         sib_copy(3, h).start()
         sib_copy(1, h).start()
 
-    for kp in range(2):
-        expand_b(0, 0, kp)
     sib_wait(0)
-    expand_a(0, 0)
     by_rows(put, (0, 256), (0, 1), (0, 1))
 
     ring_b2.forward(0)
     sib_wait(3)
-    expand_a(3, 1)
     sib_wait(1)
-    expand_a(1, 2)
     by_rows(add, (0, 256), (0, 1), (1, 2))
-    expand_b(3, 1, 0)
-    expand_b(1, 2, 0)
     by_rows(put, (256, 512), (0,), (0, 3))
 
     ring_b2.forward(1)
     for h in range(2):
         ring_a.wait_opposite(h)
         sib_copy(2, h).start()
-    expand_b(3, 1, 1)
-    expand_b(1, 2, 1)
     by_rows(add, (256, 512), (1,), (0, 3))
 
     sib_wait(2)
-    expand_a(2, 3)
 
     def finish_three(rows, lanes, value):
         total = (acc[rows, lanes] + value).astype(jnp.bfloat16)
@@ -422,7 +425,6 @@
     opposite = (q + 2) % 4
 
     ring_b2.wait_opposite(0)
-    expand_b(2, 3, 0)
     by_rows(put, (768, 256), (0,), (0, 4))
 
     @pl.when(core == 0)
@@ -435,7 +437,6 @@
         finish_pair(1 - opposite // 2)
 
     ring_b2.wait_opposite(1)
-    expand_b(2, 3, 1)
 
     def finish_last(rows, lanes, value):
         narrow[opposite, rows] = (acc[rows, lanes] + value).astype(jnp.bfloat16)
@@ -481,13 +482,12 @@
             pltpu.SMEM((1,), jnp.float32),
             pltpu.SMEM((1,), jnp.float32),
             pltpu.VMEM((1, 1024), jnp.float32),
+            pltpu.SMEM((512,), jnp.int32),
             *[pltpu.VMEM((32, 2, HALF, 128), bf16)] * 2,
             *[pltpu.VMEM((8, 2, TILE, 128), bf16)] * 2,
             *[pltpu.VMEM((4, cap1, TILE, 128), bf16)] * 2,
             *[pltpu.VMEM((2, 2, capa + 1, HALF, 128), bf16)] * 4,
             *[pltpu.VMEM((capb + 1, TILE, 128), bf16)] * 8,
-            pltpu.VMEM((1024, 4096), bf16),
-            pltpu.VMEM((1024, 4096), bf16),
             pltpu.VMEM((1024, 1024), jnp.float32),
             pltpu.VMEM((4, 1024, 256), bf16),
             pltpu.VMEM((1024, 1024), jnp.float32),

time: 60.9 us -> 57.1 us (0.938)
  Pallas kernels: 58 us -> 54.1 us
    pallas_call x1, Pallas kernels: 55.3 us -> 51.4 us  [contract(): pl.pallas_call(functools.partial(comm_kernel, cap1, capa, capb), out_shap...]
where the time goes in v4:
time: 57.1 us; the launch traced here: 56.9 us
  Pallas kernels  54.1 us (95%)
  local copies, waits for them, and re-layouts  1.32 us (2%)
  loops' own time  0.74 us (1%)
  between operations  0.67 us (1%)
    pallas_call x1, Pallas kernels, contract(): pl.pallas_call(functools.partial(comm_kernel, cap1, capa, capb), out_shap...  51.4 us
    pallas_call x1, Pallas kernels, tables(): pl.pallas_call(table_kernel, out_shape=(jax.ShapeDtypeStruct((192,), jnp....  2.7 us
    unnamed x1, local copies, waits for them, and re-layouts  1.32 us

profile of v4, /device:TPU:1, one launch (start us, length us, event | category | flops | bytes accessed | tf_op | source)
XLA Modules:
  0.0 56.9 jit_solution(1167073735022470766)
XLA Ops:
  0.0 2.7 %shard_map.77 = (s32[192]{0:T(256)S(1)}, s32[1]{0:T(128)}) custom-call(s32[16,16]{1,0:T(8,128)} %mask_a.1, s32[16,16]{1,0:T(8,128)} %mask_b.1), custom_call_target="tpu_custom_call" | custom-call | tf_op jit(solution)/shard_map/pallas_call | solution.py:95
  3.4 52.2 %conditional.1 = (bf16[1,1,1024,1024]{3,2,1,0:T(8,128)(2,1)S(1)}) conditional(s32[]{:T(128)} %bitcast.4, (s32[192]{0:T(256)S(1)}, s32[16,16]{1,0:T(8,128)}, s32[16,16]{1,0:T(8,128)}, f32[1]{0:T(128)}, f32[1]{0:T(128)}, /*index=5*/f32[1,1024]{1,0:T(1,128)}, bf16[16,4,64,128]{3,2,1,0:T(8,128)(2,1)}, ...), branch_computations={%region_0.0_spmd, %region_1.0_spmd, %region_2.0_spmd, %region_3.0_... | conditional | bytes 8 | solution.py:510
  3.6 51.4 %branch_1_fun.1 = bf16[1024,1024]{1,0:T(8,128)(2,1)S(1)} custom-call(s32[192]{0:T(256)S(1)} %get-tuple-element.83.tab_in, s32[16,16]{1,0:T(8,128)} %get-tuple-element.84.mask_a_in, s32[16,16]{1,0:T(8,128)} %get-tuple-element.85.mask_b_in, f32[1]{0:T(128)} %get-tuple-element.86.occ_i_in, f32[1]{0:T(128)} %get-tuple-element.87.occ_j_in, ...), custom_call_target="tpu_custom_call" | custom-call | tf_op jit(solution)/shard_map/cond/branch_1_fun/pallas_call | solution.py:473
  55.5 1.3 %copy.17 = bf16[1,1,1024,1024]{3,2,1,0:T(8,128)(2,1)} copy(bf16[1,1,1024,1024]{3,2,1,0:T(8,128)(2,1)S(1)} %get-tuple-element.111) | data formatting | bytes 4194304
